TPU v7x, 32 devices: a whole 2x2x4 slice. The times are simulated.
32 devices in a mesh: dp: 8 (over z, y), expert: 4 (over x, core).
Axes of the slice: x: 2, y: 2, z: 4, core: 2. Of those that a mesh axis runs over, the one named last changes fastest.
Arguments:
- tokens: bfloat16 [4096, 1024], P(('dp', 'expert')), may hold values from -6 to 6
- cotangent: bfloat16 [4096, 1024], P(('dp', 'expert')), may hold values from -6 to 6
- expert_ids: int32 [4096, 2], P(('dp', 'expert')), may hold values from 0 to 3, all different within a row; in each aligned block of 128 rows (0 to 127, 128 to 255, ...) at most 128 rows name the same one
- gate_weights: float32 [4096, 2], P(('dp', 'expert')), may hold values from 0.05 to 1
- w_gate: bfloat16 [4, 384, 1024], P('expert'), may hold values from -0.1875 to 0.1875
- w_up: bfloat16 [4, 384, 1024], P('expert'), may hold values from -0.1875 to 0.1875
- w_down: bfloat16 [4, 384, 1024], P('expert'), may hold values from -0.3125 to 0.3125
Outputs:
- layer_out: bfloat16 [4096, 1024], P(('dp', 'expert'))
- grad_tokens: bfloat16 [4096, 1024], P(('dp', 'expert'))
- grad_up: float32 [4, 384, 1024], P('expert', 'dp')
- grad_down: float32 [4, 384, 1024], P('expert', 'dp')
Inputs may be any that keep to these rules, and one draw needn't show every extreme that they name: `expert_ids`: each row names 2 different experts. Among the 128 rows of one device no expert is named more than 128 times, and in every draw some expert is named exactly 128 times by the rows of some device.
All inputs are finite; a program needn't handle non-finite values.
Results may differ from a plain program's by a relative error of at most 0.0065.
Values may be sent and summed in bfloat16 or wider, within the bound.
A program may use at most 64 MiB of HBM per device.

v0:
```python
import jax
import jax.numpy as jnp
from jax import lax
from jax.sharding import PartitionSpec as P


def batched(left_op, right_op, left_dim, right_dim):
    return lax.dot_general(
        left_op,
        right_op,
        (((left_dim,), (right_dim,)), ((0,), (0,))),
        preferred_element_type=jnp.float32,
    )


def forward(received, w_gate, w_up, w_down):
    gate_pre = batched(received, w_gate, 2, 2)
    up_pre = batched(received, w_up, 2, 2)
    gate_sig = jax.nn.sigmoid(gate_pre)
    hidden = (gate_pre * gate_sig * up_pre).astype(jnp.bfloat16)
    expert_out = batched(hidden, w_down, 2, 1).astype(jnp.bfloat16)
    return ((gate_pre, up_pre, gate_sig, hidden), expert_out)


def backward(received, grad_out, saved_acts, w_gate, w_up, w_down):
    gate_pre, up_pre, gate_sig, hidden = saved_acts
    grad_lower = lax.psum_scatter(
        batched(hidden, grad_out, 1, 1), "dp", scatter_dimension=1, tiled=True
    )
    grad_hidden = batched(grad_out, w_down, 2, 2)
    grad_up_pre = (grad_hidden * gate_pre * gate_sig).astype(jnp.bfloat16)
    grad_gate_pre = (grad_hidden * up_pre * gate_sig * (1.0 + gate_pre * (1.0 - gate_sig))).astype(
        jnp.bfloat16
    )
    grad_input = (batched(grad_gate_pre, w_gate, 2, 1) + batched(grad_up_pre, w_up, 2, 1)).astype(
        jnp.bfloat16
    )
    grad_upper = batched(grad_up_pre, received, 1, 1)
    grad_upper = lax.psum_scatter(grad_upper, "dp", scatter_dimension=1, tiled=True)
    return (grad_input, (grad_upper, grad_lower))


def shards(tokens, cotangent, expert_ids, gate_weights, w_gate, w_up, w_down):
    tok_rows, model_width = tokens.shape
    top_count = expert_ids.shape[1]
    local_experts = w_gate.shape[0]
    groups = lax.axis_size("expert")
    experts = local_experts * groups
    capacity = 2 * tok_rows * top_count // experts
    pair_count = tok_rows * top_count
    slot_count = experts * capacity
    flat_ids = expert_ids.reshape(-1)
    flat_gates = gate_weights.reshape(-1)
    onehot = (flat_ids[:, None] == jnp.arange(experts, dtype=jnp.int32)[None, :]).astype(jnp.int32)
    before = jnp.cumsum(onehot, axis=0) - onehot
    slot_rank = jnp.sum(before * onehot, axis=1)
    position = flat_ids * capacity + slot_rank
    matches = position[None, :] == jnp.arange(slot_count, dtype=jnp.int32)[:, None]
    source = (
        jnp.sum(jnp.where(matches, jnp.arange(pair_count, dtype=jnp.int32)[None, :] + 1, 0), axis=1)
        - 1
    )
    filled = source >= 0
    clipped = jnp.maximum(source, 0)
    token_rows = clipped // top_count
    slot_gates = jnp.where(filled, flat_gates[clipped], 0.0)
    sent_tokens = jnp.where(filled[:, None], tokens[token_rows], jnp.zeros((), jnp.bfloat16))
    sent_tokens = sent_tokens.reshape(experts, capacity, model_width)
    sent_grads = (slot_gates[:, None] * cotangent[token_rows].astype(jnp.float32)).astype(
        jnp.bfloat16
    )
    sent_grads = sent_grads.reshape(experts, capacity, model_width)
    received = lax.all_to_all(sent_tokens, "expert", split_axis=0, concat_axis=1, tiled=True)
    saved_acts, expert_out = forward(received, w_gate, w_up, w_down)
    back_out = lax.all_to_all(expert_out, "expert", split_axis=1, concat_axis=0, tiled=True)
    grad_out = lax.all_to_all(sent_grads, "expert", split_axis=0, concat_axis=1, tiled=True)
    grad_input, grads = backward(received, grad_out, saved_acts, w_gate, w_up, w_down)
    back_grad = lax.all_to_all(grad_input, "expert", split_axis=1, concat_axis=0, tiled=True)
    out_rows = (
        back_out.reshape(slot_count, model_width)[position].astype(jnp.float32)
        * flat_gates[:, None]
    )
    layer_out = jnp.sum(out_rows.reshape(tok_rows, top_count, model_width), axis=1).astype(
        jnp.bfloat16
    )
    grad_rows = back_grad.reshape(slot_count, model_width)[position].astype(jnp.float32)
    grad_tokens = jnp.sum(grad_rows.reshape(tok_rows, top_count, model_width), axis=1).astype(
        jnp.bfloat16
    )
    grad_scale = (tok_rows * lax.axis_size("dp") * groups * top_count / experts) ** (-0.5)
    return (layer_out, grad_tokens, grads[0] * grad_scale, grads[1] * grad_scale)


def solution(mesh):
    in_specs = (
        P(("dp", "expert"), None),
        P(("dp", "expert"), None),
        P(("dp", "expert"), None),
        P(("dp", "expert"), None),
        P("expert", None, None),
        P("expert", None, None),
        P("expert", None, None),
    )
    out_specs = (
        P(("dp", "expert"), None),
        P(("dp", "expert"), None),
        P("expert", "dp", None),
        P("expert", "dp", None),
    )
    return jax.shard_map(shards, mesh=mesh, in_specs=in_specs, out_specs=out_specs, check_vma=False)
```

profile of v0, /device:TPU:0, one launch (start us, length us, event | category | flops | bytes accessed | tf_op | source)
XLA Modules:
  0.0 203.4 jit_solution(15513453985991420824)
XLA Ops:
  7.2 0.0 copy-start
  7.2 0.9 copy.39
  8.1 0.1 eq.39
  8.2 0.1 reshape.250
  8.4 1.2 reduce-window.6
  9.6 0.1 slice.18
  9.7 0.1 copy.41
  9.8 0.1 copy.42
  9.9 0.1 add_bitcast_fusion
  10.0 0.2 select_reduce_fusion
  10.2 0.8 copy.45
  11.0 0.1 reshape.257
  11.1 3.5 %gather_fusion.2 = f32[512]{0:T(512)S(1)} fusion(f32[256]{0:T(256)S(1)} %reshape.257, s32[1024]{0:T(1024)S(1)} %pad_clamp_fusion), kind=kCustom, calls=%fused_computation.2 | custom fusion | bytes 6144 | tf_op jit(solution)/shard_map/gather | solution.py:66
  14.7 2.1 %gather_fusion = bf16[512,1024]{1,0:T(8,128)(2,1)S(1)} fusion(bf16[128,1024]{1,0:T(8,128)(2,1)S(1)} %copy-done.1, s32[1024]{0:T(1024)S(1)} %pad_clamp_fusion.2), kind=kCustom, calls=%fused_computation | custom fusion | bytes 2099200 | tf_op jit(solution)/shard_map/gather | solution.py:67
  16.8 1.2 broadcast_select_fusion
  18.0 4.2 %all-to-all-start = ((bf16[4,128,1024]{2,1,0:T(8,128)(2,1)}), bf16[4,128,1024]{2,1,0:T(8,128)(2,1)S(1)}, u32[]{:S(2)}, u32[]{:S(2)}) async-start(bf16[4,128,1024]{2,1,0:T(8,128)(2,1)} %broadcast_select_fusion), calls=%async_computation | async-start | bytes 2097152 | tf_op jit(solution)/shard_map/all_to_all | solution.py:73
  22.2 2.0 %gather_fusion.3 = bf16[512,1024]{1,0:T(8,128)(2,1)S(1)} fusion(bf16[128,1024]{1,0:T(8,128)(2,1)S(1)} %copy-done.2, s32[1024]{0:T(1024)S(1)} %pad_clamp_fusion.2), kind=kCustom, calls=%fused_computation.3 | custom fusion | bytes 2099200 | tf_op jit(solution)/shard_map/gather | solution.py:69
  24.3 1.2 fusion
  25.5 11.1 %all-to-all-done = bf16[4,128,1024]{2,1,0:T(8,128)(2,1)S(1)} async-done(((bf16[4,128,1024]{2,1,0:T(8,128)(2,1)}), bf16[4,128,1024]{2,1,0:T(8,128)(2,1)S(1)}, u32[]{:S(2)}, u32[]{:S(2)}) %all-to-all-start) | async-done | bytes 1048608 | tf_op jit(solution)/shard_map/all_to_all | solution.py:73
  36.6 3.5 %all-to-all-start.2 = ((bf16[4,128,1024]{2,1,0:T(8,128)(2,1)}), bf16[4,128,1024]{2,1,0:T(8,128)(2,1)S(1)}, u32[]{:S(2)}, u32[]{:S(2)}) async-start(bf16[4,128,1024]{2,1,0:T(8,128)(2,1)} %fusion), calls=%async_computation.2 | async-start | bytes 2097152 | tf_op jit(solution)/shard_map/all_to_all | solution.py:76
  40.1 0.0 reduce-scatter.5.cloned.1.call-start
  40.2 0.0 copy-start.3
  40.2 2.9 %fusion.11 = f32[512,384]{1,0:T(8,128)} fusion(bf16[512,1024]{1,0:T(8,128)(2,1)S(1)} %bitcast.83, bf16[1,384,1024]{2,1,0:T(8,128)(2,1)} %param.11), kind=kOutput, calls=%fused_computation.25 | convolution fusion | flops 402653184 | bytes 2621440 | tf_op jit(solution)/shard_map/dot_general | solution.py:8
  43.1 1.6 fusion.7
  44.7 9.8 %all-to-all-done.2 = bf16[4,128,1024]{2,1,0:T(8,128)(2,1)S(1)} async-done(((bf16[4,128,1024]{2,1,0:T(8,128)(2,1)}), bf16[4,128,1024]{2,1,0:T(8,128)(2,1)S(1)}, u32[]{:S(2)}, u32[]{:S(2)}) %all-to-all-start.2) | async-done | bytes 1048608 | tf_op jit(solution)/shard_map/all_to_all | solution.py:76
  54.5 3.0 %multiply_convert_fusion = (bf16[512,384]{1,0:T(8,128)(2,1)S(1)}, bf16[512,384]{1,0:T(8,128)(2,1)S(1)}, f32[512,384]{1,0:T(8,128)}) fusion(f32[512,384]{1,0:T(8,128)} %fusion.11, f32[512,384]{1,0:T(8,128)} %fusion.7, bf16[512,1024]{1,0:T(8,128)(2,1)S(1)} %bitcast.92, bf16[1,384,1024]{2,1,0:T(8,128)(2,1)S(1)} %copy-done), kind=kOutput, calls=%fused_computation.27 | convolution fusion | flops 404422656 | bytes 4980736 | tf_op jit(solution)/shard_map/dot_general | solution.py:8
  57.5 0.8 copy-done.5
  58.3 1.8 convolution_bitcast_fusion
  60.1 0.0 reduce-scatter.5.cloned.1.call-update
  60.1 0.2 reduce-scatter.3.cloned.1.call-start
  60.3 0.0 copy-start.7
  60.4 1.7 convolution_bitcast_fusion.1
  62.1 0.0 reduce-scatter.3.cloned.1.call-update
  62.1 0.0 copy-start.4
  62.1 2.6 %fusion.9 = f32[512,1024]{1,0:T(8,128)S(1)} fusion(bf16[1,384,1024]{2,1,0:T(8,128)(2,1)S(1)} %copy-done.7, f32[512,384]{1,0:T(8,128)} %fusion.11, f32[512,384]{1,0:T(8,128)} %get-tuple-element.10, f32[512,384]{1,0:T(8,128)} %fusion.7), kind=kOutput, calls=%fused_computation.23 | convolution fusion | flops 404619264 | bytes 5242880 | tf_op jit(solution)/shard_map/dot_general | solution.py:8
  64.7 0.7 fusion.2
  65.4 1.6 copy.58
  67.1 0.5 broadcast.255
  67.6 7.8 %reduce.2 = bf16[512,1024]{1,0:T(8,128)(2,1)} reduce(bf16[512,1,1024]{2,1,0:T(2,128)(2,1)S(1)} %bitcast.88, bf16[]{:T(256)} %broadcast.255), dimensions={1}, to_apply=%bitcast.79.reduce_sub_computation | reduce | bytes 2097154
  75.4 3.8 %reshape.318 = bf16[4,2,65536]{2,1,0:T(2,128)(2,1)} reshape(bf16[512,1024]{1,0:T(8,128)(2,1)} %reduce.2) | data formatting | bytes 2097152
  79.2 4.5 %all-to-all-start.3 = ((bf16[4,2,65536]{2,1,0:T(2,128)(2,1)}), bf16[4,2,65536]{2,1,0:T(2,128)(2,1)}, u32[]{:S(2)}, u32[]{:S(2)}) async-start(bf16[4,2,65536]{2,1,0:T(2,128)(2,1)} %reshape.318), calls=%async_computation.3 | async-start | bytes 2097152 | tf_op jit(solution)/shard_map/all_to_all | solution.py:78
  83.7 0.7 fusion.1
  84.4 1.6 copy.59
  86.0 7.8 %reduce.1 = bf16[512,1024]{1,0:T(8,128)(2,1)} reduce(bf16[512,1,1024]{2,1,0:T(2,128)(2,1)S(1)} %bitcast.89, bf16[]{:T(256)} %broadcast.255), dimensions={1}, to_apply=%bitcast.80.reduce_sub_computation | reduce | bytes 2097154
  93.8 3.7 %reshape.316 = bf16[4,2,65536]{2,1,0:T(2,128)(2,1)} reshape(bf16[512,1024]{1,0:T(8,128)(2,1)} %reduce.1) | data formatting | bytes 2097152
  97.6 0.3 all-to-all-done.3
  97.9 3.8 %all-to-all-start.1 = ((bf16[4,2,65536]{2,1,0:T(2,128)(2,1)}), bf16[4,2,65536]{2,1,0:T(2,128)(2,1)S(1)}, u32[]{:S(2)}, u32[]{:S(2)}) async-start(bf16[4,2,65536]{2,1,0:T(2,128)(2,1)} %reshape.316), calls=%async_computation.1 | async-start | bytes 2097152 | tf_op jit(solution)/shard_map/all_to_all | solution.py:75
  101.7 0.1 copy.44
  101.9 0.1 mul.90
  102.0 4.0 %reshape.319 = bf16[512,1,1024]{2,1,0:T(2,128)(2,1)} reshape(bf16[4,2,65536]{2,1,0:T(2,128)(2,1)} %all-to-all-done.3) | data formatting | bytes 2097152
  106.0 2.0 copy.56
  108.0 1.2 gather_fusion.4
  109.1 0.2 gather.28
  109.4 6.5 %all-to-all-done.1 = bf16[4,2,65536]{2,1,0:T(2,128)(2,1)S(1)} async-done(((bf16[4,2,65536]{2,1,0:T(2,128)(2,1)}), bf16[4,2,65536]{2,1,0:T(2,128)(2,1)S(1)}, u32[]{:S(2)}, u32[]{:S(2)}) %all-to-all-start.1) | async-done | bytes 1048608 | tf_op jit(solution)/shard_map/all_to_all | solution.py:75
  115.9 2.3 %reshape.317 = bf16[512,1,1024]{2,1,0:T(2,128)(2,1)} reshape(bf16[4,2,65536]{2,1,0:T(2,128)(2,1)S(1)} %all-to-all-done.1) | data formatting | bytes 2097152
  118.2 2.0 copy.57
  120.2 1.2 gather_fusion.1
  121.3 0.7 reshape.260
  122.0 2.1 %reduce_sum.45 = bf16[128,1024]{1,0:T(8,128)(2,1)} reduce(bf16[128,2,1024]{2,1,0:T(2,128)(2,1)S(1)} %gather.28, bf16[]{:T(256)} %constant.37.clone.1), dimensions={1}, to_apply=%region_5.6 | reduce | flops 131072 | bytes 786434 | tf_op jit(solution)/shard_map/reduce_sum | solution.py:87
  124.1 2.1 %multiply_reduce_fusion = bf16[128,1024]{1,0:T(8,128)(2,1)} fusion(f32[128,2,1024]{2,1,0:T(2,128)S(1)} %reshape.260, f32[128,2]{1,0:T(8,128)S(1)} %copy.45), kind=kLoop, calls=%fused_computation.15 | loop fusion | flops 393216 | bytes 1311744 | tf_op jit(solution)/shard_map/reduce_sum | solution.py:83
  126.2 0.9 reduce-scatter.5.cloned.1.call-done
  127.1 1.6 broadcast_multiply_fusion
  128.7 66.2 %reduce-scatter.3.cloned.1.call-done = f32[1,48,1024]{2,1,0:T(8,128)} async-done(((f32[1,384,1024]{2,1,0:T(8,128)}), f32[1,48,1024]{2,1,0:T(8,128)}) %reduce-scatter.3.cloned.1.call-update) | async-done | bytes 196624 | tf_op jit(solution)/shard_map/reduce_scatter | solution.py:39
  194.9 1.6 broadcast_multiply_fusion.1
  (27 shorter events, 0.2 us)
Async XLA Ops:
  7.2 47.4 %copy-start = (bf16[1,384,1024]{2,1,0:T(8,128)(2,1)S(1)}, bf16[1,384,1024]{2,1,0:T(8,128)(2,1)}, u32[]{:S(2)}) copy-start(bf16[1,384,1024]{2,1,0:T(8,128)(2,1)} %param.13) | copy-start | bytes 2359300
  7.2 7.5 %copy-start.1 = (bf16[128,1024]{1,0:T(8,128)(2,1)S(1)}, bf16[128,1024]{1,0:T(8,128)(2,1)}, u32[]{:S(2)}) copy-start(bf16[128,1024]{1,0:T(8,128)(2,1)} %param.7) | copy-start | bytes 786436
  16.8 5.4 %copy-start.2 = (bf16[128,1024]{1,0:T(8,128)(2,1)S(1)}, bf16[128,1024]{1,0:T(8,128)(2,1)}, u32[]{:S(2)}) copy-start(bf16[128,1024]{1,0:T(8,128)(2,1)} %param.8) | copy-start | bytes 786436
  18.0 18.7 %all-to-all-start = ((bf16[4,128,1024]{2,1,0:T(8,128)(2,1)}), bf16[4,128,1024]{2,1,0:T(8,128)(2,1)S(1)}, u32[]{:S(2)}, u32[]{:S(2)}) async-start(bf16[4,128,1024]{2,1,0:T(8,128)(2,1)} %broadcast_select_fusion), calls=%async_computation | async-start | bytes 2097152 | tf_op jit(solution)/shard_map/all_to_all | solution.py:73
  36.6 17.9 %all-to-all-start.2 = ((bf16[4,128,1024]{2,1,0:T(8,128)(2,1)}), bf16[4,128,1024]{2,1,0:T(8,128)(2,1)S(1)}, u32[]{:S(2)}, u32[]{:S(2)}) async-start(bf16[4,128,1024]{2,1,0:T(8,128)(2,1)} %fusion), calls=%async_computation.2 | async-start | bytes 2097152 | tf_op jit(solution)/shard_map/all_to_all | solution.py:76
  40.1 86.9 %reduce-scatter.5.cloned.1.call-start = ((), (), s32[]{:S(2)}) async-start(), calls=%async_computation.7 | async-start | bytes 1769472 | tf_op jit(solution)/shard_map/reduce_scatter | solution.py:27
  40.2 2.9 %copy-start.3 = (bf16[1,384,1024]{2,1,0:T(8,128)(2,1)S(1)}, bf16[1,384,1024]{2,1,0:T(8,128)(2,1)}, u32[]{:S(2)}) copy-start(bf16[1,384,1024]{2,1,0:T(8,128)(2,1)} %param.12) | copy-start | bytes 2359300
  57.5 0.8 copy-start.5
  60.1 134.8 %reduce-scatter.3.cloned.1.call-start = ((), (), s32[]{:S(2)}) async-start(), calls=%async_computation.6 | async-start | bytes 1769472 | tf_op jit(solution)/shard_map/reduce_scatter | solution.py:39
  60.3 1.8 copy-start.7
  62.1 2.6 %copy-start.4 = (bf16[1,384,1024]{2,1,0:T(8,128)(2,1)S(1)}, bf16[1,384,1024]{2,1,0:T(8,128)(2,1)}, u32[]{:S(2)}) copy-start(bf16[1,384,1024]{2,1,0:T(8,128)(2,1)} %param.12) | copy-start | bytes 2359300
  75.4 8.3 %copy-start.6 = (bf16[512,384]{1,0:T(8,128)(2,1)S(1)}, bf16[512,384]{1,0:T(8,128)(2,1)}, u32[]{:S(2)}) copy-start(bf16[512,384]{1,0:T(8,128)(2,1)} %copy-done.5) | copy-start | bytes 1179652
  79.2 18.8 %all-to-all-start.3 = ((bf16[4,2,65536]{2,1,0:T(2,128)(2,1)}), bf16[4,2,65536]{2,1,0:T(2,128)(2,1)}, u32[]{:S(2)}, u32[]{:S(2)}) async-start(bf16[4,2,65536]{2,1,0:T(2,128)(2,1)} %reshape.318), calls=%async_computation.3 | async-start | bytes 2097152 | tf_op jit(solution)/shard_map/all_to_all | solution.py:78
  93.8 7.9 %copy-start.8 = (s32[128,2]{0,1:T(2,128)S(1)}, s32[128,2]{0,1:T(2,128)}, u32[]{:S(2)}) copy-start(s32[128,2]{0,1:T(2,128)} %param.9) | copy-start | bytes 3076
  97.9 17.9 %all-to-all-start.1 = ((bf16[4,2,65536]{2,1,0:T(2,128)(2,1)}), bf16[4,2,65536]{2,1,0:T(2,128)(2,1)S(1)}, u32[]{:S(2)}, u32[]{:S(2)}) async-start(bf16[4,2,65536]{2,1,0:T(2,128)(2,1)} %reshape.316), calls=%async_computation.1 | async-start | bytes 2097152 | tf_op jit(solution)/shard_map/all_to_all | solution.py:75
Sparse Core Ops, SparseCore 0:
  60.2 66.8 reduce-scatter.4
  130.5 64.3 reduce-scatter.2
where the time goes:
time: 204 us; the launch traced here: 203 us
  waiting for transfers between devices  95 us (47%)
  local copies, waits for them, and re-layouts  35.7 us (18%)
  other arithmetic  27 us (13%)
  starting transfers between devices  16.3 us (8%)
  matrix products  15 us (7%)
  between operations  14.3 us (7%)
    reduce_scatter x1, waiting for transfers between devices, backward(): lax.psum_scatter(grad_upper, 'dp', scatter_dimension=1, tiled=True)  66.2 us
    unnamed x27, local copies, waits for them, and re-layouts  20.8 us
    unnamed x3, other arithmetic  15.7 us
    dot_general x8, matrix products, batched(): lax.dot_general(left_op, right_op, (((left_dim,), (right_dim,)), ((0,), (...  15 us
    all_to_all x1, waiting for transfers between devices, shards(): lax.all_to_all(sent_tokens, 'expert', split_axis=0, concat_axis=1, tiled=...  11.1 us
    all_to_all x1, waiting for transfers between devices, shards(): lax.all_to_all(sent_grads, 'expert', split_axis=0, concat_axis=1, tiled=T...  9.83 us
    all_to_all x1, waiting for transfers between devices, shards(): lax.all_to_all(expert_out, 'expert', split_axis=1, concat_axis=0, tiled=T...  6.51 us
    all_to_all x1, starting transfers between devices, shards(): lax.all_to_all(grad_input, 'expert', split_axis=1, concat_axis=0, tiled=T...  4.48 us
  transfers between devices with their start and end apart: 6, of which 6 were waited for; matrix products, arithmetic and copies ran while one was open for 29% of the time, Pallas kernels for 0%

commit v1 on v0

v1 whole, which is shorter than its diff:
```python
import functools

import jax
import jax.numpy as jnp
from jax import lax
from jax.experimental import pallas as pl
from jax.experimental.pallas import tpu as pltpu
from jax.sharding import PartitionSpec as P

MESH = pl.DeviceIdType.MESH
F32 = jnp.float32
BF16 = jnp.bfloat16


def dot_nn(a, b):
    return lax.dot_general(a, b, (((1,), (0,)), ((), ())), preferred_element_type=F32)


def dot_nt(a, b):
    return lax.dot_general(a, b, (((1,), (1,)), ((), ())), preferred_element_type=F32)


def layer_kernel(cfg, tok_hbm, cot_hbm, gates_ref, wg_hbm, wu_hbm, wd_hbm,
                 out_ref, gtok_ref, gup_ref, gdn_ref,
                 wg, wu, wd, xb, cb, gts, gob, hT, guT, silu_s, q_s, ggp_s, gup_s,
                 part, pre, pre_send, ret, gbuf, yrecv, zsend, zrecv,
                 local_sem, xs, xr, ps, pr, rs, rr, ts, tr, qs, qr, us, ur, ys, yr, zs, zr):
    chips, outer, fused, scale = cfg
    T, D = tok_hbm.shape
    H = wg.shape[0]
    R2 = 2 * T
    dp = lax.axis_index("dp")
    ex = lax.axis_index("expert")
    core = lax.rem(ex, 2)
    chip = lax.div(ex, 2)
    partner = (dp, chip * 2 + 1 - core)

    def ahead(d):
        return (dp, lax.rem(chip + d, chips) * 2 + core)

    def behind(d):
        return (dp, lax.rem(chip + chips - d, chips) * 2 + core)

    yi = lax.rem(dp, 2)
    zo = lax.div(dp, 2)
    ypeer = (zo * 2 + 1 - yi, ex)

    def zahead(d):
        return (lax.rem(zo + d, outer) * 2 + yi, ex)

    def remote(src, dst, ssem, rsem, dev):
        return pltpu.make_async_remote_copy(src_ref=src, dst_ref=dst, send_sem=ssem, recv_sem=rsem,
                                            device_id=dev, device_id_type=MESH)

    locals_ = [
        pltpu.make_async_copy(tok_hbm, xb.at[0], local_sem.at[0]),
        pltpu.make_async_copy(wg_hbm.at[0], wg, local_sem.at[1]),
        pltpu.make_async_copy(wu_hbm.at[0], wu, local_sem.at[2]),
        pltpu.make_async_copy(wd_hbm.at[0], wd, local_sem.at[3]),
        pltpu.make_async_copy(cot_hbm, cb.at[0], local_sem.at[4]),
    ]
    for c in locals_:
        c.start()

    peers = [partner] + [ahead(d) for d in range(1, chips)]
    if fused:
        peers = peers + [ypeer] + [zahead(d) for d in range(1, outer)]
    barrier = pltpu.get_barrier_semaphore()
    for dev in peers:
        pl.semaphore_signal(barrier, inc=1, device_id=dev, device_id_type=MESH)
    pl.semaphore_wait(barrier, len(peers))

    pending = []

    def go(c):
        c.start()
        pending.append(c)
        return c

    srcs = [gates_ref, tok_hbm, cot_hbm]
    bufs = [gts, xb, cb]
    xin, pin, rin = {}, {}, {}
    for t in range(3):
        for d in range(1, chips):
            xin[t, d] = go(remote(srcs[t], bufs[t].at[2 * d], xs.at[t, d], xr.at[t, d], ahead(d)))
        if t < 2:
            pin[t] = go(remote(srcs[t], bufs[t].at[1], ps.at[t], pr.at[t], partner))
    pin[2] = go(remote(srcs[2], bufs[2].at[1], ps.at[2], pr.at[2], partner))

    def relay(t):
        for d in range(1, chips):
            xin[t, d].wait_recv()
            rin[t, d] = go(remote(bufs[t].at[2 * d], bufs[t].at[2 * d + 1], rs.at[t, d], rr.at[t, d], partner))

    eye = lax.broadcasted_iota(jnp.int32, (T, T), 0) == lax.broadcasted_iota(jnp.int32, (T, T), 1)

    def gate_col(p):
        cols = []
        for s in (2 * p, 2 * p + 1):
            row = gates_ref[pl.ds(ex, 1), :] if s == 0 else gts[s, pl.ds(ex, 1), :]
            cols.append(jnp.sum(jnp.where(eye, row, 0.0), axis=1, keepdims=True))
        return jnp.concatenate(cols, axis=0)

    def forward(p):
        rows = pl.ds(p * R2, R2)
        x = xb[2 * p:2 * p + 2].reshape(R2, D)
        gp = dot_nt(x, wg[...])
        up = dot_nt(x, wu[...])
        sig = jax.nn.sigmoid(gp)
        silu = gp * sig
        hidden = (silu * up).astype(BF16)
        silu_s[rows, :] = silu
        q_s[rows, :] = up * sig * (1.0 + gp * (1.0 - sig))
        hT[:, rows] = hidden.T
        return hidden

    def forward_out(p, hidden):
        eo = gate_col(p) * dot_nn(hidden, wd[...])
        part[0, 2 * p:2 * p + 2] = eo.astype(BF16).reshape(2, T, D)

    def weighted(p):
        go_ = gate_col(p) * cb[2 * p:2 * p + 2].reshape(R2, D).astype(F32)
        gob[pl.ds(p * R2, R2), :] = go_.astype(BF16)

    def backward(p):
        rows = pl.ds(p * R2, R2)
        gh = dot_nt(gob[rows, :], wd[...])
        gu = (gh * silu_s[rows, :]).astype(BF16)
        gup_s[rows, :] = gu
        ggp_s[rows, :] = (gh * q_s[rows, :]).astype(BF16)
        guT[:, rows] = gu.T

    def backward_in(p):
        rows = pl.ds(p * R2, R2)
        gi = dot_nn(ggp_s[rows, :], wg[...]) + dot_nn(gup_s[rows, :], wu[...])
        part[1, 2 * p:2 * p + 2] = gi.astype(BF16).reshape(2, T, D)

    locals_[0].wait()
    locals_[1].wait()
    locals_[2].wait()
    pin[0].wait_recv()
    pin[1].wait_recv()
    hidden = forward(0)
    locals_[3].wait()
    forward_out(0, hidden)
    tin, qin, uin = {}, {}, {}
    tin[0] = go(remote(part.at[0, 1], ret.at[0, 0], ts.at[0], tr.at[0], partner))
    relay(0)
    locals_[4].wait()
    pin[2].wait_recv()
    weighted(0)
    backward(0)
    relay(1)
    backward_in(0)
    tin[1] = go(remote(part.at[1, 1], ret.at[1, 0], ts.at[1], tr.at[1], partner))

    def hand_over(k):
        for d in range(1, chips):
            qin[k, d] = go(remote(part.at[k, 2 * d + 1], pre.at[k, d], qs.at[k, d], qr.at[k, d], partner))

    def send_back(k):
        for d in range(1, chips):
            qin[k, d].wait_recv()
            pre_send[k, d] = (part[k, 2 * d].astype(F32) + pre[k, d].astype(F32)).astype(BF16)
            uin[k, d] = go(remote(pre_send.at[k, d], ret.at[k, d], us.at[k, d], ur.at[k, d], behind(d)))

    for d in range(1, chips):
        rin[0, d].wait_recv()
        rin[1, d].wait_recv()
        forward_out(d, forward(d))
    hand_over(0)
    relay(2)
    for d in range(1, chips):
        rin[2, d].wait_recv()
        weighted(d)

    yin, zin = {}, {}

    def weight_grad(k, left, right, full_ref):
        tile = 256 if D % 256 == 0 else D
        for n in range(D // tile):
            cols = pl.ds(n * tile, tile)
            g = dot_nn(left[...], right(cols))
            if fused:
                gbuf[k, :, :, :, cols] = g.astype(BF16).reshape(gbuf.shape[1:4] + (tile,))
            else:
                full_ref[:, cols] = g * scale
        if fused:
            for d in list(range(1, outer)) + [0]:
                yin[k, d] = go(remote(gbuf.at[k, lax.rem(zo + d, outer), 1 - yi], yrecv.at[k, d],
                                      ys.at[k, d], yr.at[k, d], ypeer))

    def outer_step(k):
        for d in range(1, outer):
            yin[k, d].wait_recv()
            zsend[k, d] = (gbuf[k, lax.rem(zo + d, outer), yi].astype(F32) + yrecv[k, d].astype(F32)).astype(BF16)
            zin[k, d] = go(remote(zsend.at[k, d], zrecv.at[k, d], zs.at[k, d], zr.at[k, d], zahead(d)))

    def outer_end(k, ref):
        yin[k, 0].wait_recv()
        total = gbuf[k, zo, yi].astype(F32) + yrecv[k, 0].astype(F32)
        for d in range(1, outer):
            zin[k, d].wait_recv()
            total = total + zrecv[k, d].astype(F32)
        ref[...] = total * scale

    weight_grad(0, hT, lambda cols: gob[:, cols], gdn_ref)
    for d in range(1, chips):
        backward(d)
    weight_grad(1, guT, lambda cols: jnp.concatenate([xb[s, :, cols] for s in range(2 * chips)], axis=0), gup_ref)
    send_back(0)
    for d in range(1, chips):
        backward_in(d)
    hand_over(1)
    send_back(1)
    if fused:
        outer_step(0)
        outer_step(1)

    def collect(k, ref):
        total = part[k, 0].astype(F32)
        tin[k].wait_recv()
        total = total + ret[k, 0].astype(F32)
        for d in range(1, chips):
            uin[k, d].wait_recv()
            total = total + ret[k, d].astype(F32)
        ref[...] = total.astype(BF16)

    collect(0, out_ref)
    collect(1, gtok_ref)
    if fused:
        outer_end(0, gdn_ref)
        outer_end(1, gup_ref)
    for c in pending:
        c.wait_send()


def shards(tokens, cotangent, expert_ids, gate_weights, w_gate, w_up, w_down):
    T, D = tokens.shape
    local_experts, H, _ = w_gate.shape
    groups = lax.axis_size("expert")
    dps = lax.axis_size("dp")
    experts = groups * local_experts
    assert local_experts == 1 and groups % 2 == 0
    chips = groups // 2
    piece = H // dps
    fused = dps % 2 == 0 and piece % 16 == 0
    outer = dps // 2 if fused else 1
    top = expert_ids.shape[1]
    scale = (T * dps * groups * top / experts) ** (-0.5)
    erows = -(-experts // 8) * 8
    gates = jnp.sum(
        jnp.where(expert_ids[None, :, :] == jnp.arange(erows, dtype=jnp.int32)[:, None, None],
                  gate_weights[None, :, :], 0.0), axis=2)
    R = groups * T
    grad_shape = (piece, D) if fused else (H, D)
    gp = piece if fused else 16
    vm = pltpu.VMEM
    dma = pltpu.SemaphoreType.DMA
    anyspec = pl.BlockSpec(memory_space=pl.ANY)
    vspec = pl.BlockSpec(memory_space=pltpu.VMEM)
    layer_out, grad_tokens, gup, gdn = pl.pallas_call(
        functools.partial(layer_kernel, (chips, outer, fused, scale)),
        out_shape=(
            jax.ShapeDtypeStruct((T, D), BF16),
            jax.ShapeDtypeStruct((T, D), BF16),
            jax.ShapeDtypeStruct(grad_shape, F32),
            jax.ShapeDtypeStruct(grad_shape, F32),
        ),
        in_specs=[anyspec, anyspec, vspec, anyspec, anyspec, anyspec],
        out_specs=(vspec, vspec, vspec, vspec),
        scratch_shapes=[
            vm((H, D), BF16), vm((H, D), BF16), vm((H, D), BF16),
            vm((groups, T, D), BF16), vm((groups, T, D), BF16), vm((groups, erows, T), F32),
            vm((R, D), BF16), vm((H, R), BF16), vm((H, R), BF16),
            vm((R, H), F32), vm((R, H), F32), vm((R, H), BF16), vm((R, H), BF16),
            vm((2, groups, T, D), BF16), vm((2, chips, T, D), BF16), vm((2, chips, T, D), BF16),
            vm((2, chips, T, D), BF16),
            vm((2, outer, 2, gp, D), BF16), vm((2, outer, gp, D), BF16),
            vm((2, outer, gp, D), BF16), vm((2, outer, gp, D), BF16),
            dma((5,)),
            dma((3, chips)), dma((3, chips)), dma((3,)), dma((3,)), dma((3, chips)), dma((3, chips)),
            dma((2,)), dma((2,)), dma((2, chips)), dma((2, chips)), dma((2, chips)), dma((2, chips)),
            dma((2, outer)), dma((2, outer)), dma((2, outer)), dma((2, outer)),
        ],
        compiler_params=pltpu.CompilerParams(collective_id=0, has_side_effects=True,
                                             vmem_limit_bytes=60 * 1024 * 1024),
        name="moe_layer",
    )(tokens, cotangent, gates, w_gate, w_up, w_down)
    if not fused:
        gup = lax.psum_scatter(gup, "dp", scatter_dimension=0, tiled=True)
        gdn = lax.psum_scatter(gdn, "dp", scatter_dimension=0, tiled=True)
    return layer_out, grad_tokens, gup[None], gdn[None]


def solution(mesh):
    both = P(("dp", "expert"), None)
    weights = P("expert", None, None)
    return jax.shard_map(
        shards,
        mesh=mesh,
        in_specs=(both, both, both, both, weights, weights, weights),
        out_specs=(both, both, P("expert", "dp", None), P("expert", "dp", None)),
        check_vma=False,
    )
```

time: 204 us -> 50.9 us (0.25)
  waiting for transfers between devices: 95 us -> 0 us
  Pallas kernels: 0 us -> 44.3 us
  local copies, waits for them, and re-layouts: 35.7 us -> 4.41 us
  other arithmetic: 27 us -> 1.29 us
  starting transfers between devices: 16.3 us -> 0 us
  matrix products: 15 us -> 0 us
  between operations: 14.3 us -> 0.65 us
    reduce_scatter x2 -> x0, waiting for transfers between devices: 67.1 us -> none  [the longest x1 66.2 us: backward(): lax.psum_scatter(grad_upper, 'dp', scatter_dimension=1, tiled=True)]
    pallas_call x0 -> x1, Pallas kernels: none -> 44.3 us  [shards(): pl.pallas_call(functools.partial(layer_kernel, (chips, outer, fused, scal...]
    all_to_all x4 -> x0, waiting for transfers between devices: 27.8 us -> none  [the longest x1 11.1 us: shards(): lax.all_to_all(sent_tokens, 'expert', split_axis=0, concat_axis=1, tiled=...]
    unnamed x27 -> x10, local copies, waits for them, and re-layouts: 20.8 us -> 4.41 us
    all_to_all x4 -> x0, starting transfers between devices: 16 us -> none  [the longest x1 4.48 us: shards(): lax.all_to_all(grad_input, 'expert', split_axis=1, concat_axis=0, tiled=T...]
    unnamed x3 -> x0, other arithmetic: 15.7 us -> none
    dot_general x8 -> x0, matrix products: 15 us -> none  [batched(): lax.dot_general(left_op, right_op, (((left_dim,), (right_dim,)), ((0,), (...]
    gather x6 -> x0, local copies, waits for them, and re-layouts: 10.1 us -> none  [the longest x1 3.51 us: shards(): slot_gates = jnp.where(filled, flat_gates[clipped], 0.0)]
  transfers between devices with their start and end apart: 6 -> 0, of which waited for: 6 -> 0; matrix products, arithmetic and copies ran while one was open for 29% -> 0% of each run, Pallas kernels for 0% -> 0%
where the time goes in v1:
time: 50.9 us; the launch traced here: 50.6 us
  Pallas kernels  44.3 us (87%)
  local copies, waits for them, and re-layouts  4.41 us (9%)
  other arithmetic  1.29 us (3%)
  between operations  0.65 us (1%)
    pallas_call x1, Pallas kernels, shards(): pl.pallas_call(functools.partial(layer_kernel, (chips, outer, fused, scal...  44.3 us
    unnamed x10, local copies, waits for them, and re-layouts  4.41 us
    reduce_sum x1, other arithmetic, shards(): jnp.sum(jnp.where(expert_ids[None, :, :] == jnp.arange(erows, dtype=jnp.i...  1.29 us

profile of v1, /device:TPU:0, one launch (start us, length us, event | category | flops | bytes accessed | tf_op | source)
XLA Modules:
  0.0 50.6 jit_solution(18221121166414569156)
XLA Ops:
  0.6 1.3 %select_reduce_fusion.gates_ref = f32[8,128]{1,0:T(8,128)} fusion(f32[128,2]{0,1:T(2,128)} %param.10, s32[128,2]{0,1:T(2,128)} %param.9), kind=kLoop, calls=%fused_computation | loop fusion | flops 5120 | bytes 6144 | tf_op jit(solution)/shard_map/reduce_sum | solution.py:252
  1.9 44.3 %moe_layer.1 = (bf16[128,1024]{1,0:T(8,128)(2,1)}, bf16[128,1024]{1,0:T(8,128)(2,1)}, f32[48,1024]{1,0:T(8,128)}, f32[48,1024]{1,0:T(8,128)}) custom-call(bf16[128,1024]{1,0:T(8,128)(2,1)} %tok_hbm.1, bf16[128,1024]{1,0:T(8,128)(2,1)} %cot_hbm.1, f32[8,128]{1,0:T(8,128)} %select_reduce_fusion.gates_ref, bf16[1,384,1024]{2,1,0:T(8,128)(2,1)} %wg_hbm.1, ...), custom_call_target="tpu_custom_call" | custom-call | tf_op jit(solution)/shard_map/moe_layer/pallas_call | solution.py:262
  46.2 0.0 copy-start
  46.2 1.7 %copy.17 = bf16[128,1024]{1,0:T(8,128)(2,1)} copy(bf16[128,1024]{1,0:T(8,128)(2,1)} %get-tuple-element.16) | data formatting | bytes 524288
  47.9 0.0 copy-done
  47.9 0.0 copy-start.2
  47.9 0.7 %copy.18 = bf16[128,1024]{1,0:T(8,128)(2,1)} copy(bf16[128,1024]{1,0:T(8,128)(2,1)S(1)} %copy-done) | data formatting | bytes 524288
  48.6 0.3 copy-done.2
  49.0 0.0 copy-start.1
  49.0 0.7 %copy.19 = f32[1,48,1024]{2,1,0:T(8,128)} copy(f32[1,48,1024]{2,1,0:T(8,128)S(1)} %bitcast.3) | data formatting | bytes 393216
  49.6 0.3 copy-done.1
  50.0 0.7 %copy.20 = f32[1,48,1024]{2,1,0:T(8,128)} copy(f32[1,48,1024]{2,1,0:T(8,128)S(1)} %bitcast.2) | data formatting | bytes 393216
Async XLA Ops:
  46.2 1.7 %copy-start = (bf16[128,1024]{1,0:T(8,128)(2,1)S(1)}, bf16[128,1024]{1,0:T(8,128)(2,1)}, u32[]{:S(2)}) copy-start(bf16[128,1024]{1,0:T(8,128)(2,1)} %get-tuple-element.17) | copy-start | bytes 786436
  47.9 1.0 %copy-start.2 = (f32[48,1024]{1,0:T(8,128)S(1)}, f32[48,1024]{1,0:T(8,128)}, u32[]{:S(2)}) copy-start(f32[48,1024]{1,0:T(8,128)} %get-tuple-element.10) | copy-start | bytes 589828
  49.0 1.0 %copy-start.1 = (f32[48,1024]{1,0:T(8,128)S(1)}, f32[48,1024]{1,0:T(8,128)}, u32[]{:S(2)}) copy-start(f32[48,1024]{1,0:T(8,128)} %get-tuple-element.11) | copy-start | bytes 589828

commit v2 on v1

--- a/solution.py
+++ b/solution.py
@@ -20,9 +20,9 @@
     return lax.dot_general(a, b, (((1,), (1,)), ((), ())), preferred_element_type=F32)
 
 
-def layer_kernel(cfg, tok_hbm, cot_hbm, gates_ref, wg_hbm, wu_hbm, wd_hbm,
+def layer_kernel(cfg, tok_hbm, cot_hbm, ids_ref, gw_ref, wg_hbm, wu_hbm, wd_hbm,
                  out_ref, gtok_ref, gup_ref, gdn_ref,
-                 wg, wu, wd, xb, cb, gts, gob, hT, guT, silu_s, q_s, ggp_s, gup_s,
+                 wg, wu, wd, xb, cb, gates_ref, gts, gob, hT, guT, silu_s, q_s, ggp_s, gup_s,
                  part, pre, pre_send, ret, gbuf, yrecv, zsend, zrecv,
                  local_sem, xs, xr, ps, pr, rs, rr, ts, tr, qs, qr, us, ur, ys, yr, zs, zr):
     chips, outer, fused, scale = cfg
@@ -45,8 +45,14 @@
     zo = lax.div(dp, 2)
     ypeer = (zo * 2 + 1 - yi, ex)
 
-    def zahead(d):
-        return (lax.rem(zo + d, outer) * 2 + yi, ex)
+    levels = outer.bit_length() - 1
+
+    def flipped(m):
+        z = zo
+        for b in range(levels):
+            if (m >> b) & 1:
+                z = z + (1 << b) * (1 - 2 * lax.rem(lax.div(zo, 1 << b), 2))
+        return z
 
     def remote(src, dst, ssem, rsem, dev):
         return pltpu.make_async_remote_copy(src_ref=src, dst_ref=dst, send_sem=ssem, recv_sem=rsem,
@@ -62,9 +68,15 @@
     for c in locals_:
         c.start()
 
+    ranks = lax.broadcasted_iota(jnp.int32, gates_ref.shape, 0)
+    table = jnp.zeros(gates_ref.shape, F32)
+    for k in range(ids_ref.shape[0]):
+        table = table + jnp.where(ids_ref[pl.ds(k, 1), :] == ranks, gw_ref[pl.ds(k, 1), :], 0.0)
+    gates_ref[...] = table
+
     peers = [partner] + [ahead(d) for d in range(1, chips)]
     if fused:
-        peers = peers + [ypeer] + [zahead(d) for d in range(1, outer)]
+        peers = peers + [ypeer] + [(flipped(1 << b) * 2 + yi, ex) for b in range(levels)]
     barrier = pltpu.get_barrier_semaphore()
     for dev in peers:
         pl.semaphore_signal(barrier, inc=1, device_id=dev, device_id_type=MESH)
@@ -175,6 +187,7 @@
         weighted(d)
 
     yin, zin = {}, {}
+    order = sorted(range(outer), key=lambda m: (m & -m) if m else outer)
 
     def weight_grad(k, left, right, full_ref):
         tile = 256 if D % 256 == 0 else D
@@ -186,23 +199,28 @@
             else:
                 full_ref[:, cols] = g * scale
         if fused:
-            for d in list(range(1, outer)) + [0]:
-                yin[k, d] = go(remote(gbuf.at[k, lax.rem(zo + d, outer), 1 - yi], yrecv.at[k, d],
-                                      ys.at[k, d], yr.at[k, d], ypeer))
-
-    def outer_step(k):
-        for d in range(1, outer):
-            yin[k, d].wait_recv()
-            zsend[k, d] = (gbuf[k, lax.rem(zo + d, outer), yi].astype(F32) + yrecv[k, d].astype(F32)).astype(BF16)
-            zin[k, d] = go(remote(zsend.at[k, d], zrecv.at[k, d], zs.at[k, d], zr.at[k, d], zahead(d)))
+            for m in order:
+                yin[k, m] = go(remote(gbuf.at[k, flipped(m), 1 - yi], yrecv.at[k, m],
+                                      ys.at[k, m], yr.at[k, m], ypeer))
+
+    def halve(k, b):
+        for m in order:
+            if (m & -m) == 1 << b:
+                total = level_sum(k, m, b)
+                zsend[k, m] = total.astype(BF16)
+                zin[k, m] = go(remote(zsend.at[k, m], zrecv.at[k, m], zs.at[k, m], zr.at[k, m],
+                                      (flipped(1 << b) * 2 + yi, ex)))
+
+    def level_sum(k, m, b):
+        yin[k, m].wait_recv()
+        total = gbuf[k, flipped(m), yi].astype(F32) + yrecv[k, m].astype(F32)
+        for a in range(b):
+            zin[k, m + (1 << a)].wait_recv()
+            total = total + zrecv[k, m + (1 << a)].astype(F32)
+        return total
 
     def outer_end(k, ref):
-        yin[k, 0].wait_recv()
-        total = gbuf[k, zo, yi].astype(F32) + yrecv[k, 0].astype(F32)
-        for d in range(1, outer):
-            zin[k, d].wait_recv()
-            total = total + zrecv[k, d].astype(F32)
-        ref[...] = total * scale
+        ref[...] = level_sum(k, 0, levels) * scale
 
     weight_grad(0, hT, lambda cols: gob[:, cols], gdn_ref)
     for d in range(1, chips):
@@ -212,10 +230,14 @@
     for d in range(1, chips):
         backward_in(d)
     hand_over(1)
+    if fused and levels > 0:
+        halve(0, 0)
     send_back(1)
     if fused:
-        outer_step(0)
-        outer_step(1)
+        for b in range(1, levels):
+            halve(0, b)
+        for b in range(levels):
+            halve(1, b)
 
     def collect(k, ref):
         total = part[k, 0].astype(F32)
@@ -233,6 +255,15 @@
         outer_end(1, gup_ref)
     for c in pending:
         c.wait_send()
+
+
+def write_out(a, b, c, d, out_a, out_b, out_c, out_d, sem):
+    copies = [pltpu.make_async_copy(src, dst, sem.at[i])
+              for i, (src, dst) in enumerate([(a, out_a), (b, out_b), (c, out_c), (d, out_d)])]
+    for c in copies:
+        c.start()
+    for c in copies:
+        c.wait()
 
 
 def shards(tokens, cotangent, expert_ids, gate_weights, w_gate, w_up, w_down):
@@ -244,14 +275,11 @@
     assert local_experts == 1 and groups % 2 == 0
     chips = groups // 2
     piece = H // dps
-    fused = dps % 2 == 0 and piece % 16 == 0
+    fused = dps % 2 == 0 and piece % 16 == 0 and (dps & (dps - 1)) == 0
     outer = dps // 2 if fused else 1
     top = expert_ids.shape[1]
     scale = (T * dps * groups * top / experts) ** (-0.5)
     erows = -(-experts // 8) * 8
-    gates = jnp.sum(
-        jnp.where(expert_ids[None, :, :] == jnp.arange(erows, dtype=jnp.int32)[:, None, None],
-                  gate_weights[None, :, :], 0.0), axis=2)
     R = groups * T
     grad_shape = (piece, D) if fused else (H, D)
     gp = piece if fused else 16
@@ -262,16 +290,16 @@
     layer_out, grad_tokens, gup, gdn = pl.pallas_call(
         functools.partial(layer_kernel, (chips, outer, fused, scale)),
         out_shape=(
-            jax.ShapeDtypeStruct((T, D), BF16),
-            jax.ShapeDtypeStruct((T, D), BF16),
-            jax.ShapeDtypeStruct(grad_shape, F32),
-            jax.ShapeDtypeStruct(grad_shape, F32),
+            vm((T, D), BF16),
+            vm((T, D), BF16),
+            vm(grad_shape, F32),
+            vm(grad_shape, F32),
         ),
-        in_specs=[anyspec, anyspec, vspec, anyspec, anyspec, anyspec],
+        in_specs=[anyspec, anyspec, vspec, vspec, anyspec, anyspec, anyspec],
         out_specs=(vspec, vspec, vspec, vspec),
         scratch_shapes=[
             vm((H, D), BF16), vm((H, D), BF16), vm((H, D), BF16),
-            vm((groups, T, D), BF16), vm((groups, T, D), BF16), vm((groups, erows, T), F32),
+            vm((groups, T, D), BF16), vm((groups, T, D), BF16), vm((erows, T), F32), vm((groups, erows, T), F32),
             vm((R, D), BF16), vm((H, R), BF16), vm((H, R), BF16),
             vm((R, H), F32), vm((R, H), F32), vm((R, H), BF16), vm((R, H), BF16),
             vm((2, groups, T, D), BF16), vm((2, chips, T, D), BF16), vm((2, chips, T, D), BF16),
@@ -286,10 +314,20 @@
         compiler_params=pltpu.CompilerParams(collective_id=0, has_side_effects=True,
                                              vmem_limit_bytes=60 * 1024 * 1024),
         name="moe_layer",
-    )(tokens, cotangent, gates, w_gate, w_up, w_down)
+    )(tokens, cotangent, expert_ids.T, gate_weights.T, w_gate, w_up, w_down)
     if not fused:
         gup = lax.psum_scatter(gup, "dp", scatter_dimension=0, tiled=True)
         gdn = lax.psum_scatter(gdn, "dp", scatter_dimension=0, tiled=True)
+        return layer_out, grad_tokens, gup[None], gdn[None]
+    results = [pltpu.with_memory_space_constraint(r, pltpu.VMEM) for r in (layer_out, grad_tokens, gup, gdn)]
+    layer_out, grad_tokens, gup, gdn = pl.pallas_call(
+        write_out,
+        out_shape=tuple(jax.ShapeDtypeStruct(r.shape, r.dtype) for r in results),
+        in_specs=[vspec] * 4,
+        out_specs=(anyspec,) * 4,
+        scratch_shapes=[dma((4,))],
+        name="write_out",
+    )(*results)
     return layer_out, grad_tokens, gup[None], gdn[None]
 
 

time: 50.9 us -> 48.4 us (0.951)
  local copies, waits for them, and re-layouts: 4.41 us -> 0 us
  Pallas kernels: 44.3 us -> 47.6 us
  other arithmetic: 1.29 us -> 0 us
    unnamed x10 -> x0, local copies, waits for them, and re-layouts: 4.41 us -> none
    pallas_call x1, Pallas kernels: 44.3 us -> 46.7 us  [shards(): pl.pallas_call(functools.partial(layer_kernel, (chips, outer, fused, scal...]
    reduce_sum x1 -> x0, other arithmetic: 1.29 us -> none  [shards(): jnp.sum(jnp.where(expert_ids[None, :, :] == jnp.arange(erows, dtype=jnp.i...]
    pallas_call x0 -> x1, Pallas kernels: none -> 0.95 us  [shards(): pl.pallas_call(write_out, out_shape=tuple((jax.ShapeDtypeStruct(r.shape,...]
where the time goes in v2:
time: 48.4 us; the launch traced here: 48.2 us
  Pallas kernels  47.6 us (98%)
  between operations  0.64 us (1%)
    pallas_call x1, Pallas kernels, shards(): pl.pallas_call(functools.partial(layer_kernel, (chips, outer, fused, scal...  46.7 us

profile of v2, /device:TPU:0, one launch (start us, length us, event | category | flops | bytes accessed | tf_op | source)
XLA Modules:
  0.0 48.2 jit_solution(1884929754822603473)
XLA Ops:
  0.6 46.7 %moe_layer.1 = (bf16[128,1024]{1,0:T(8,128)(2,1)S(1)}, bf16[128,1024]{1,0:T(8,128)(2,1)S(1)}, f32[48,1024]{1,0:T(8,128)S(1)}, f32[48,1024]{1,0:T(8,128)S(1)}) custom-call(bf16[128,1024]{1,0:T(8,128)(2,1)} %tok_hbm.1, bf16[128,1024]{1,0:T(8,128)(2,1)} %cot_hbm.1, s32[2,128]{1,0:T(2,128)} %bitcast.4, f32[2,128]{1,0:T(2,128)} %bitcast.5, ...), custom_call_target="tpu_custom_call" | custom-call | tf_op jit(solution)/shard_map/moe_layer/pallas_call | solution.py:290
  47.3 1.0 %write_out.1 = (bf16[128,1024]{1,0:T(8,128)(2,1)}, bf16[128,1024]{1,0:T(8,128)(2,1)}, f32[48,1024]{1,0:T(8,128)}, f32[48,1024]{1,0:T(8,128)}) custom-call(bf16[128,1024]{1,0:T(8,128)(2,1)S(1)} %get-tuple-element.12.a, bf16[128,1024]{1,0:T(8,128)(2,1)S(1)} %get-tuple-element.13.b, f32[48,1024]{1,0:T(8,128)S(1)} %get-tuple-element.14.c, ...), custom_call_target="tpu_custom_call" | custom-call | tf_op jit(solution)/shard_map/write_out/pallas_call | solution.py:323

commit v3 on v2

--- a/solution.py
+++ b/solution.py
@@ -187,7 +187,7 @@
         weighted(d)
 
     yin, zin = {}, {}
-    order = sorted(range(outer), key=lambda m: (m & -m) if m else outer)
+    order = sorted(range(outer), key=lambda m: ((m & -m) if m else outer, -m))
 
     def weight_grad(k, left, right, full_ref):
         tile = 256 if D % 256 == 0 else D

time: 48.4 us -> 46.9 us (0.969)
  Pallas kernels: 47.6 us -> 46.1 us
    pallas_call x1, Pallas kernels: 46.7 us -> 45.1 us  [shards(): pl.pallas_call(functools.partial(layer_kernel, (chips, outer, fused, scal...]
where the time goes in v3:
time: 46.9 us; the launch traced here: 46.7 us
  Pallas kernels  46.1 us (98%)
  between operations  0.64 us (1%)
    pallas_call x1, Pallas kernels, shards(): pl.pallas_call(functools.partial(layer_kernel, (chips, outer, fused, scal...  45.1 us
    pallas_call x1, Pallas kernels, shards(): pl.pallas_call(write_out, out_shape=tuple((jax.ShapeDtypeStruct(r.shape,...  0.95 us

profile of v3, /device:TPU:0, one launch (start us, length us, event | category | flops | bytes accessed | tf_op | source)
XLA Modules:
  0.0 46.7 jit_solution(1088738314904632511)
XLA Ops:
  0.6 45.1 %moe_layer.1 = (bf16[128,1024]{1,0:T(8,128)(2,1)S(1)}, bf16[128,1024]{1,0:T(8,128)(2,1)S(1)}, f32[48,1024]{1,0:T(8,128)S(1)}, f32[48,1024]{1,0:T(8,128)S(1)}) custom-call(bf16[128,1024]{1,0:T(8,128)(2,1)} %tok_hbm.1, bf16[128,1024]{1,0:T(8,128)(2,1)} %cot_hbm.1, s32[2,128]{1,0:T(2,128)} %bitcast.4, f32[2,128]{1,0:T(2,128)} %bitcast.5, ...), custom_call_target="tpu_custom_call" | custom-call | tf_op jit(solution)/shard_map/moe_layer/pallas_call | solution.py:290
  45.8 1.0 %write_out.1 = (bf16[128,1024]{1,0:T(8,128)(2,1)}, bf16[128,1024]{1,0:T(8,128)(2,1)}, f32[48,1024]{1,0:T(8,128)}, f32[48,1024]{1,0:T(8,128)}) custom-call(bf16[128,1024]{1,0:T(8,128)(2,1)S(1)} %get-tuple-element.12.a, bf16[128,1024]{1,0:T(8,128)(2,1)S(1)} %get-tuple-element.13.b, f32[48,1024]{1,0:T(8,128)S(1)} %get-tuple-element.14.c, ...), custom_call_target="tpu_custom_call" | custom-call | tf_op jit(solution)/shard_map/write_out/pallas_call | solution.py:323

commit v4 on v3

--- a/solution.py
+++ b/solution.py
@@ -199,9 +199,9 @@
             else:
                 full_ref[:, cols] = g * scale
         if fused:
-            for m in order:
-                yin[k, m] = go(remote(gbuf.at[k, flipped(m), 1 - yi], yrecv.at[k, m],
-                                      ys.at[k, m], yr.at[k, m], ypeer))
+            for j, m in [(k, m) for m in order[:-1]] + [(0, 0), (1, 0)] * k:
+                yin[j, m] = go(remote(gbuf.at[j, flipped(m), 1 - yi], yrecv.at[j, m],
+                                      ys.at[j, m], yr.at[j, m], ypeer))
 
     def halve(k, b):
         for m in order:

time: 46.9 us -> 44.8 us (0.955)
  Pallas kernels: 46.1 us -> 44 us
    pallas_call x1, Pallas kernels: 45.1 us -> 43 us  [shards(): pl.pallas_call(functools.partial(layer_kernel, (chips, outer, fused, scal...]
where the time goes in v4:
time: 44.8 us; the launch traced here: 44.6 us
  Pallas kernels  44 us (98%)
  between operations  0.64 us (1%)
    pallas_call x1, Pallas kernels, shards(): pl.pallas_call(functools.partial(layer_kernel, (chips, outer, fused, scal...  43 us
    pallas_call x1, Pallas kernels, shards(): pl.pallas_call(write_out, out_shape=tuple((jax.ShapeDtypeStruct(r.shape,...  0.95 us

profile of v4, /device:TPU:0, one launch (start us, length us, event | category | flops | bytes accessed | tf_op | source)
XLA Modules:
  0.0 44.6 jit_solution(7365629493892379411)
XLA Ops:
  0.6 43.0 %moe_layer.1 = (bf16[128,1024]{1,0:T(8,128)(2,1)S(1)}, bf16[128,1024]{1,0:T(8,128)(2,1)S(1)}, f32[48,1024]{1,0:T(8,128)S(1)}, f32[48,1024]{1,0:T(8,128)S(1)}) custom-call(bf16[128,1024]{1,0:T(8,128)(2,1)} %tok_hbm.1, bf16[128,1024]{1,0:T(8,128)(2,1)} %cot_hbm.1, s32[2,128]{1,0:T(2,128)} %bitcast.4, f32[2,128]{1,0:T(2,128)} %bitcast.5, ...), custom_call_target="tpu_custom_call" | custom-call | tf_op jit(solution)/shard_map/moe_layer/pallas_call | solution.py:290
  43.6 1.0 %write_out.1 = (bf16[128,1024]{1,0:T(8,128)(2,1)}, bf16[128,1024]{1,0:T(8,128)(2,1)}, f32[48,1024]{1,0:T(8,128)}, f32[48,1024]{1,0:T(8,128)}) custom-call(bf16[128,1024]{1,0:T(8,128)(2,1)S(1)} %get-tuple-element.12.a, bf16[128,1024]{1,0:T(8,128)(2,1)S(1)} %get-tuple-element.13.b, f32[48,1024]{1,0:T(8,128)S(1)} %get-tuple-element.14.c, ...), custom_call_target="tpu_custom_call" | custom-call | tf_op jit(solution)/shard_map/write_out/pallas_call | solution.py:323
